TPU v7x, 32 devices: a whole 2x2x4 slice. The times are simulated.
32 devices in a mesh: segment: 4 (over x, core), dp: 4 (over z), tensor: 2 (over y).
Axes of the slice: x: 2, y: 2, z: 4, core: 2. Of those that a mesh axis runs over, the one named last changes fastest.
Arguments:
- acts: bfloat16 [4, 256, 1024], P('segment', ('dp', 'tensor')), may hold values from -6 to 6
- norm_gain: float32 [4, 1024], P('segment'), may hold values from 0.1 to 1.9
- final_gain: float32 [1024], replicated, may hold values from 0.1 to 1.9
- w_query: bfloat16 [4, 1024, 8192], P('segment', None, 'tensor'), may hold values from -0.015625 to 0.015625
- w_key: bfloat16 [4, 1024, 8192], P('segment', None, 'tensor'), may hold values from -0.1875 to 0.1875
- w_value: bfloat16 [4, 1024, 8192], P('segment', None, 'tensor'), may hold values from -0.1875 to 0.1875
- w_out: bfloat16 [4, 8192, 1024], P('segment', 'tensor'), may hold values from -0.0625 to 0.0625
- cache: bfloat16 [4, 2, 256, 8192], P('segment', None, 'dp', 'tensor'), may hold values from -6 to 6
Outputs:
- updated: bfloat16 [4, 256, 1024], P('segment', ('dp', 'tensor'))
- fresh: bfloat16 [4, 2, 256, 8192], P('segment', None, 'dp', 'tensor')
All inputs are finite; a program needn't handle non-finite values.
Results may differ from a plain program's by a relative error of at most 0.01.
Values may be sent and summed in bfloat16 or wider, within the bound.
A program may use at most 64 MiB of HBM per device.

v0:
```python
import jax
import jax.numpy as jnp
from jax import lax
from jax.sharding import PartitionSpec as P

HDIM = 128


EPSILON = 1e-06


def from_behind(x, axis, by):
    devices = lax.axis_size(axis)
    pairs = [(i, i + by) for i in range(devices) if 0 <= i + by < devices]
    return lax.ppermute(x, axis, pairs)


def normalize(values, gain):
    wide = values.astype(jnp.float32)
    scale = lax.rsqrt(jnp.mean(wide * wide, axis=-1, keepdims=True) + EPSILON)
    return (wide * scale * gain).astype(jnp.bfloat16)


def attend(queries, keys, values):
    length = queries.shape[0]
    heads = queries.shape[1] // HDIM
    query_heads = queries.reshape(length, heads, HDIM)
    key_heads = keys.reshape(keys.shape[0], heads, HDIM)
    value_heads = values.reshape(values.shape[0], heads, HDIM)
    scores = jnp.einsum("qhd,khd->hqk", query_heads, key_heads, preferred_element_type=jnp.float32)
    weights = jnp.exp(scores)
    probs = (weights / jnp.sum(weights, axis=-1, keepdims=True)).astype(jnp.bfloat16)
    context = jnp.einsum("hqk,khd->qhd", probs, value_heads, preferred_element_type=jnp.float32)
    return context.reshape(length, heads * HDIM).astype(jnp.bfloat16)


def project_pair(source, w_key, w_value):
    made_keys = jnp.dot(source, w_key, preferred_element_type=jnp.float32).astype(jnp.bfloat16)
    made_values = jnp.dot(source, w_value, preferred_element_type=jnp.float32).astype(jnp.bfloat16)
    return (made_keys, made_values)


def on_device(acts, norm_gain, final_gain, w_query, w_key, w_value, w_out, cache):
    tokens = acts[0]
    segment = lax.axis_index("segment")
    half = lax.axis_size("segment") // 2
    decoder = segment >= half
    normed = normalize(tokens, norm_gain[0])
    all_rows = lax.all_gather(normed, "tensor", axis=0, tiled=True)
    queries = jnp.dot(all_rows, w_query[0], preferred_element_type=jnp.float32).astype(jnp.bfloat16)
    keys, values = lax.cond(
        decoder,
        lambda: (cache[0, 0], cache[0, 1]),
        lambda: project_pair(all_rows, w_key[0], w_value[0]),
    )
    context = attend(queries, keys, values)
    branch = lax.psum_scatter(
        jnp.dot(context, w_out[0], preferred_element_type=jnp.float32).astype(jnp.bfloat16),
        "tensor",
        scatter_dimension=0,
        tiled=True,
    ).astype(jnp.float32)
    updated = (tokens.astype(jnp.float32) + branch).astype(jnp.bfloat16)
    memory_part = normalize(updated, final_gain)
    root = half - 1
    holding = memory_part
    position = segment - root
    for level in range(half.bit_length()):
        stride = 1 << level
        arrived = from_behind(holding, "segment", stride)
        taking = (position >= stride) & (position < 2 * stride)
        holding = jnp.where(taking, arrived, holding)
    memory = lax.all_gather(holding, "tensor", axis=0, tiled=True)
    fresh_keys, fresh_values = lax.cond(
        decoder, lambda: project_pair(memory, w_key[0], w_value[0]), lambda: (keys, values)
    )
    fresh = jnp.stack([fresh_keys, fresh_values])[None]
    return (updated[None], fresh)


def solution(mesh):
    placed = (
        P("segment", ("dp", "tensor"), None),
        P("segment", None),
        P(),
        P("segment", None, "tensor"),
        P("segment", None, "tensor"),
        P("segment", None, "tensor"),
        P("segment", "tensor", None),
        P("segment", None, "dp", "tensor"),
    )
    return jax.shard_map(
        on_device,
        mesh=mesh,
        in_specs=placed,
        out_specs=(P("segment", ("dp", "tensor"), None), P("segment", None, "dp", "tensor")),
        check_vma=False,
    )
```

profile of v0, /device:TPU:2, one launch (start us, length us, event | category | flops | bytes accessed | tf_op | source)
XLA Modules:
  0.0 78.3 jit_solution(6831589581872860799)
XLA Ops:
  7.2 0.0 reduce-scatter.2.cloned.1.call-start
  7.2 1.0 %fusion.53 = f32[32]{0:T(128)S(1)} fusion(bf16[1,32,1024]{2,1,0:T(8,128)(2,1)} %param.12), kind=kLoop, calls=%fused_computation.45 | loop fusion | flops 98272 | bytes 65664 | tf_op jit(solution)/shard_map/reduce_sum | solution.py:20
  8.2 0.9 %fusion.55 = bf16[32,1024]{1,0:T(8,128)(2,1)S(1)} fusion(bf16[1,32,1024]{2,1,0:T(8,128)(2,1)} %param.12, f32[1024]{0:T(1024)} %bitcast.103, f32[32]{0:T(128)S(1)} %add_rsqrt_fusion.1), kind=kLoop, calls=%fused_computation.47 | loop fusion | flops 131072 | bytes 135296 | tf_op jit(solution)/shard_map/convert_element_type | solution.py:21
  9.1 4.9 %all_gather.6 = bf16[64,1024]{1,0:T(8,128)(2,1)S(1)} all-gather(bf16[32,1024]{1,0:T(8,128)(2,1)S(1)} %fusion.55), channel_id=1, replica_groups=mesh['segment'=4,'dp'=4,'tensor'=2] {'tensor'}, dimensions={0}, use_global_device_ids=true | all-gather | bytes 196608 | tf_op jit(solution)/shard_map/all_gather | solution.py:49
  14.1 1.3 %conditional.2 = (bf16[64,4096]{1,0:T(8,128)(2,1)S(1)}, bf16[64,4096]{1,0:T(8,128)(2,1)S(1)}) conditional(s32[]{:T(128)} %convert_element_type.58, (bf16[1,1024,4096]{2,1,0:T(8,128)(2,1)}, bf16[64,1024]{1,0:T(8,128)(2,1)S(1)}, bf16[1,1024,4096]{2,1,0:T(8,128)(2,1)}) %tuple.36, bf16[1,2,64,4096]{3,2,1,0:T(8,128)(2,1)} %param.19), branch_computations={%region_1.0_spmd, %region_2.0_spmd} | conditional | flops 1074266112 | bytes 43253824 | solution.py:51
  14.1 1.3 %slice_bitcast_fusion = (bf16[64,4096]{1,0:T(8,128)(2,1)S(1)}, bf16[64,4096]{1,0:T(8,128)(2,1)S(1)}) fusion(bf16[1,2,64,4096]{3,2,1,0:T(8,128)(2,1)} %param.1), kind=kLoop, calls=%fused_computation.6 | loop fusion | bytes 2097152 | tf_op jit(solution)/shard_map/cond/branch_1_fun/squeeze | solution.py:53
  15.3 5.0 %fusion.33 = bf16[8,32,8,128]{3,2,1,0:T(8,128)(2,1)S(1)} fusion(bf16[64,1024]{1,0:T(8,128)(2,1)S(1)} %all_gather.6, bf16[1,1024,4096]{2,1,0:T(8,128)(2,1)} %param.15), kind=kOutput, calls=%fused_computation.23 | convolution fusion | flops 537133056 | bytes 9043968 | tf_op jit(solution)/shard_map/dot_general | solution.py:50
  20.3 0.4 convolution_exponential_fusion
  20.7 0.4 fusion.36
  21.1 0.0 copy-start
  21.1 0.0 copy-start.1
  21.1 5.6 %fusion.37 = bf16[64,1024]{1,0:T(8,128)(2,1)} fusion(bf16[1,4096,1024]{2,1,0:T(8,128)(2,1)} %param.18, bf16[32,8,8,128]{3,2,1,0:T(8,128)(2,1)S(1)} %fusion.36), kind=kOutput, calls=%fused_computation.25 | convolution fusion | flops 536936448 | bytes 9043968 | tf_op jit(solution)/shard_map/dot_general | solution.py:58
  26.7 0.0 reduce-scatter.2.cloned.1.call-update
  26.8 17.0 %reduce-scatter.2.cloned.1.call-done = bf16[32,1024]{1,0:T(8,128)(2,1)} async-done(((bf16[64,1024]{1,0:T(8,128)(2,1)}), bf16[32,1024]{1,0:T(8,128)(2,1)}) %reduce-scatter.2.cloned.1.call-update) | async-done | bytes 65552 | tf_op jit(solution)/shard_map/reduce_scatter | solution.py:57
  43.8 0.0 copy-done
  43.8 1.0 %fusion.50 = f32[32]{0:T(128)S(1)} fusion(bf16[32,1024]{1,0:T(8,128)(2,1)} %reduce-scatter.2.cloned.1.call-done, bf16[1,32,1024]{2,1,0:T(8,128)(2,1)S(1)} %copy-done), kind=kLoop, calls=%fused_computation.42 | loop fusion | flops 229344 | bytes 131200 | tf_op jit(solution)/shard_map/reduce_sum | solution.py:20
  44.7 0.0 copy-done.1
  44.7 1.5 %fusion.52 = (bf16[32,1024]{1,0:T(8,128)(2,1)S(1)}, bf16[1,32,1024]{2,1,0:T(8,128)(2,1)}) fusion(f32[1024]{0:T(1024)S(1)} %copy-done.1, f32[32]{0:T(128)S(1)} %add_rsqrt_fusion, bf16[32,1024]{1,0:T(8,128)(2,1)} %reduce-scatter.2.cloned.1.call-done, bf16[1,32,1024]{2,1,0:T(8,128)(2,1)S(1)} %copy-done), kind=kLoop, calls=%fused_computation.44 | loop fusion | flops 262144 | bytes 266368 | tf_op jit(solution)/shard_map/convert_element_type | solution.py:21
  46.2 1.9 %collective-permute-start = (bf16[32,1024]{1,0:T(8,128)(2,1)S(1)}, bf16[32,1024]{1,0:T(8,128)(2,1)S(1)}, u32[]{:S(2)}, u32[]{:S(2)}) collective-permute-start(bf16[32,1024]{1,0:T(8,128)(2,1)S(1)} %get-tuple-element.51), channel_id=1, source_target_pairs={{0,8},{8,16},{16,24},{1,9},{9,17},{17,25},{2,10},{10,18},{18,26},{... | collective-permute-start | bytes 196616 | tf_op jit(solution)/shard_map/ppermute | solution.py:15
  48.2 3.6 %collective-permute-done = bf16[32,1024]{1,0:T(8,128)(2,1)S(1)} collective-permute-done((bf16[32,1024]{1,0:T(8,128)(2,1)S(1)}, bf16[32,1024]{1,0:T(8,128)(2,1)S(1)}, u32[]{:S(2)}, u32[]{:S(2)}) %collective-permute-start) | collective-permute-done | bytes 65568 | tf_op jit(solution)/shard_map/ppermute | solution.py:15
  51.8 1.3 %collective-permute-start.1 = (bf16[32,1024]{1,0:T(8,128)(2,1)S(1)}, bf16[32,1024]{1,0:T(8,128)(2,1)S(1)}, u32[]{:S(2)}, u32[]{:S(2)}) collective-permute-start(bf16[32,1024]{1,0:T(8,128)(2,1)S(1)} %broadcast_select_fusion), channel_id=1, source_target_pairs={{0,16},{8,24},{1,17},{9,25},{2,18},{10,26},{3,19},{11,27},{4,20},{... | collective-permute-start | bytes 196616 | tf_op jit(solution)/shard_map/ppermute | solution.py:15
  53.1 4.9 %collective-permute-done.1 = bf16[32,1024]{1,0:T(8,128)(2,1)S(1)} collective-permute-done((bf16[32,1024]{1,0:T(8,128)(2,1)S(1)}, bf16[32,1024]{1,0:T(8,128)(2,1)S(1)}, u32[]{:S(2)}, u32[]{:S(2)}) %collective-permute-start.1) | collective-permute-done | bytes 65568 | tf_op jit(solution)/shard_map/ppermute | solution.py:15
  58.0 4.9 %all_gather.7 = bf16[64,1024]{1,0:T(8,128)(2,1)S(1)} all-gather(bf16[32,1024]{1,0:T(8,128)(2,1)S(1)} %broadcast_select_fusion.1), channel_id=1, replica_groups=mesh['segment'=4,'dp'=4,'tensor'=2] {'tensor'}, dimensions={0}, use_global_device_ids=true | all-gather | bytes 196608 | tf_op jit(solution)/shard_map/all_gather | solution.py:73
  62.9 7.4 %conditional.3 = (bf16[1,64,4096]{2,1,0:T(8,128)(2,1)S(1)}, bf16[1,64,4096]{2,1,0:T(8,128)(2,1)S(1)}) conditional(s32[]{:T(128)} %convert_element_type.58, (bf16[64,4096]{1,0:T(8,128)(2,1)S(1)}, bf16[64,4096]{1,0:T(8,128)(2,1)S(1)}) %conditional.2, (bf16[1,1024,4096]{2,1,0:T(8,128)(2,1)}, bf16[64,1024]{1,0:T(8,128)(2,1)S(1)}, ...), branch_computations={%region_6.7_spmd, %region_7.8_spmd} | conditional | flops 1074266112 | bytes 43253824 | solution.py:74
  62.9 0.0 slice-start
  62.9 0.0 slice-start.1
  62.9 5.1 %fusion.20 = bf16[1,64,4096]{2,1,0:T(8,128)(2,1)S(1)} fusion(bf16[64,1024]{1,0:T(8,128)(2,1)S(1)} %get-tuple-element.32, bf16[1,1024,4096]{2,1,0:T(8,128)(2,1)} %get-tuple-element.34), kind=kOutput, calls=%fused_computation.14 | convolution fusion | flops 537133056 | bytes 9043968 | tf_op jit(solution)/shard_map/cond/branch_1_fun/dot_general | solution.py:39
  68.0 0.0 slice-done
  68.0 0.7 slice-done.1
  68.8 1.6 %fusion.23 = bf16[1,64,4096]{2,1,0:T(8,128)(2,1)S(1)} fusion(bf16[64,1024]{1,0:T(8,128)(2,1)S(1)} %get-tuple-element.32, bf16[1,1024,4096]{2,1,0:T(8,128)(2,1)S(1)} %bitcast.98), kind=kOutput, calls=%fused_computation.15 | convolution fusion | flops 537133056 | bytes 9043968 | tf_op jit(solution)/shard_map/cond/branch_1_fun/dot_general | solution.py:38
  70.4 1.1 %maximum_bitcast_fusion = bf16[1,2,64,4096]{3,2,1,0:T(8,128)(2,1)} fusion(bf16[1,64,4096]{2,1,0:T(8,128)(2,1)S(1)} %get-tuple-element.48, bf16[1,64,4096]{2,1,0:T(8,128)(2,1)S(1)} %get-tuple-element.47), kind=kLoop, calls=%fused_computation.26 | loop fusion | flops 524288 | bytes 2097152 | tf_op jit(solution)/shard_map/broadcast_in_dim | solution.py:77
  (5 shorter events, 0.0 us)
Async XLA Ops:
  7.2 36.6 %reduce-scatter.2.cloned.1.call-start = ((), (), s32[]{:S(2)}) async-start(), calls=%async_computation.1 | async-start | bytes 196608 | tf_op jit(solution)/shard_map/reduce_scatter | solution.py:57
  21.1 22.7 %copy-start = (bf16[1,32,1024]{2,1,0:T(8,128)(2,1)S(1)}, bf16[1,32,1024]{2,1,0:T(8,128)(2,1)}, u32[]{:S(2)}) copy-start(bf16[1,32,1024]{2,1,0:T(8,128)(2,1)} %param.12) | copy-start | bytes 196612
  21.1 23.6 %copy-start.1 = (f32[1024]{0:T(1024)S(1)}, f32[1024]{0:T(1024)}, u32[]{:S(2)}) copy-start(f32[1024]{0:T(1024)} %param.14) | copy-start | bytes 12292
  46.2 5.6 %collective-permute-start = (bf16[32,1024]{1,0:T(8,128)(2,1)S(1)}, bf16[32,1024]{1,0:T(8,128)(2,1)S(1)}, u32[]{:S(2)}, u32[]{:S(2)}) collective-permute-start(bf16[32,1024]{1,0:T(8,128)(2,1)S(1)} %get-tuple-element.51), channel_id=1, source_target_pairs={{0,8},{8,16},{16,24},{1,9},{9,17},{17,25},{2,10},{10,18},{18,26},{... | collective-permute-start | bytes 196616 | tf_op jit(solution)/shard_map/ppermute | solution.py:15
  51.8 6.2 %collective-permute-start.1 = (bf16[32,1024]{1,0:T(8,128)(2,1)S(1)}, bf16[32,1024]{1,0:T(8,128)(2,1)S(1)}, u32[]{:S(2)}, u32[]{:S(2)}) collective-permute-start(bf16[32,1024]{1,0:T(8,128)(2,1)S(1)} %broadcast_select_fusion), channel_id=1, source_target_pairs={{0,16},{8,24},{1,17},{9,25},{2,18},{10,26},{3,19},{11,27},{4,20},{... | collective-permute-start | bytes 196616 | tf_op jit(solution)/shard_map/ppermute | solution.py:15
  62.9 5.1 %slice-start = ((s8[8388608]{0:T(1024)(128)(4,1)}), s8[4194304]{0:T(1024)(128)(4,1)S(1)}, s32[]{:S(2)}) async-start(s8[8388608]{0:T(1024)(128)(4,1)} %bitcast.97), calls=%async_computation.2 | async-start | bytes 8388608 | tf_op jit(solution)/shard_map/cond
  62.9 5.9 %slice-start.1 = ((s8[8388608]{0:T(1024)(128)(4,1)}), s8[4194304]{0:T(1024)(128)(4,1)S(1)}, s32[]{:S(2)}) async-start(s8[8388608]{0:T(1024)(128)(4,1)} %bitcast.97), calls=%async_computation.3 | async-start | bytes 8388608 | tf_op jit(solution)/shard_map/cond
Sparse Core Ops, SparseCore 0:
  26.9 16.8 reduce-scatter.1
where the time goes:
time: 78.7 us; the launch traced here: 78.3 us
  waiting for transfers between devices  25.5 us (32%)
  matrix products  18 us (23%)
  between operations  14.1 us (18%)
  blocking collectives  9.87 us (13%)
  other arithmetic  5.45 us (7%)
  starting transfers between devices  3.24 us (4%)
  local copies, waits for them, and re-layouts  2.02 us (3%)
    reduce_scatter x1, waiting for transfers between devices, on_device(): lax.psum_scatter(jnp.dot(context, w_out[0], preferred_element_type=jnp.fl...  17 us
    ppermute x2, waiting for transfers between devices, from_behind(): return lax.ppermute(x, axis, pairs)  8.5 us
    dot_general x1, matrix products, on_device(): jnp.dot(context, w_out[0], preferred_element_type=jnp.float32)  5.64 us
    dot_general x1, matrix products, project_pair(): jnp.dot(source, w_value, preferred_element_type=jnp.float32)  5.1 us
    dot_general x1, matrix products, on_device(): jnp.dot(all_rows, w_query[0], preferred_element_type=jnp.float32)  4.95 us
    all_gather x1, blocking collectives, on_device(): all_rows = lax.all_gather(normed, 'tensor', axis=0, tiled=True)  4.93 us
    all_gather x1, blocking collectives, on_device(): memory = lax.all_gather(holding, 'tensor', axis=0, tiled=True)  4.93 us
    ppermute x2, starting transfers between devices, from_behind(): return lax.ppermute(x, axis, pairs)  3.2 us
  transfers between devices with their start and end apart: 3, of which 3 were waited for; matrix products, arithmetic and copies ran while one was open for 0% of the time, Pallas kernels for 0%

commit v1 on v0

v1 whole, which is shorter than its diff:
```python
import functools

import jax
import jax.numpy as jnp
from jax import lax
from jax.experimental import pallas as pl
from jax.experimental.pallas import tpu as pltpu
from jax.sharding import PartitionSpec as P

HDIM = 128
EPSILON = 1e-06
MESH = pl.DeviceIdType.MESH
F32 = jnp.float32
BF16 = jnp.bfloat16


def largest(total, limit):
    width = min(total, limit)
    while total % width:
        width -= HDIM
    return width


def kernel(
    sections, split, wide, narrow,
    acts, norm_gain, final_gain, w_query, w_key, w_value, w_out, cache,
    updated, fresh,
    query_buf, key_buf, value_buf, out_buf, cache_buf, gain_buf, final_buf,
    gathered, normed, context, own_part, got_part, sent_rows, got_rows, total,
    qkv_sem, out_sem, small_sem, act_send, act_recv, part_send, part_recv, mem_send, mem_recv,
):
    segment = lax.axis_index("segment")
    me = lax.axis_index("tensor")
    half = sections // 2
    root = half - 1
    decoder = segment >= half
    encoder = segment < half
    is_root = segment == root
    not_root = segment != root
    parts, local_rows, features = gathered.shape
    rows = parts * local_rows
    groups = query_buf.shape[0]
    blocks = out_buf.shape[0]

    def columns(j):
        return pl.ds(pl.multiple_of(j * wide, wide), wide)

    def load_qkv(which, source, target, j):
        return pltpu.make_async_copy(source.at[0, :, columns(j)], target.at[j], qkv_sem.at[which, j])

    def load_q(j):
        return load_qkv(0, w_query, query_buf, j)

    def load_k(j):
        return load_qkv(1, w_key, key_buf, j)

    def load_v(j):
        return load_qkv(2, w_value, value_buf, j)

    def load_out(c):
        return pltpu.make_async_copy(w_out.at[0, :, pl.ds(c * narrow, narrow)], out_buf.at[c], out_sem.at[c])

    own_acts = pltpu.make_async_copy(acts.at[0], gathered.at[me], small_sem.at[0])
    gain_copy = pltpu.make_async_copy(norm_gain, gain_buf, small_sem.at[1])
    final_copy = pltpu.make_async_copy(final_gain, final_buf, small_sem.at[2])
    cache_copy = pltpu.make_async_copy(cache.at[0], cache_buf, small_sem.at[3])

    barrier = pltpu.get_barrier_semaphore()
    for off in range(1, split):
        pl.semaphore_signal(barrier, inc=1, device_id={"tensor": lax.rem(me + off, split)}, device_id_type=MESH)

    @pl.when(is_root)
    def _():
        for s in range(half, sections):
            pl.semaphore_signal(barrier, inc=1, device_id={"segment": s}, device_id_type=MESH)

    @pl.when(decoder)
    def _():
        pl.semaphore_signal(barrier, inc=1, device_id={"segment": root}, device_id_type=MESH)

    own_acts.start()
    gain_copy.start()
    final_copy.start()

    @pl.when(encoder)
    def _():
        def begin(j, carry):
            load_q(j).start()
            load_k(j).start()
            load_v(j).start()
            return carry

        lax.fori_loop(0, groups, begin, 0)
        for c in range(blocks):
            load_out(c).start()

    @pl.when(decoder)
    def _():
        cache_copy.start()

        def begin(j, carry):
            load_q(j).start()
            return carry

        lax.fori_loop(0, groups, begin, 0)
        for c in range(blocks):
            load_out(c).start()

        def begin_pair(j, carry):
            load_k(j).start()
            load_v(j).start()
            return carry

        lax.fori_loop(0, groups, begin_pair, 0)

    @pl.when(is_root)
    def _():
        pl.semaphore_wait(barrier, split - 1 + sections - half)

    @pl.when(decoder)
    def _():
        pl.semaphore_wait(barrier, split)

    @pl.when(encoder & not_root)
    def _():
        pl.semaphore_wait(barrier, split - 1)

    def send_acts(off):
        return pltpu.make_async_remote_copy(
            src_ref=acts.at[0],
            dst_ref=gathered.at[me],
            send_sem=act_send.at[off - 1],
            recv_sem=act_recv.at[off - 1],
            device_id={"tensor": lax.rem(me + off, split)},
            device_id_type=MESH,
        )

    def send_all_rows(off, c):
        return pltpu.make_async_remote_copy(
            src_ref=own_part.at[c],
            dst_ref=got_part.at[off - 1, c],
            send_sem=part_send.at[off - 1, c],
            recv_sem=part_recv.at[off - 1, c],
            device_id={"tensor": lax.rem(me + off, split)},
            device_id_type=MESH,
        )

    def send_their_rows(off, c):
        peer = lax.rem(me + off, split)
        return pltpu.make_async_remote_copy(
            src_ref=own_part.at[c, peer],
            dst_ref=got_part.at[off - 1, c, peer],
            send_sem=part_send.at[off - 1, c],
            recv_sem=part_recv.at[off - 1, c],
            device_id={"tensor": peer},
            device_id_type=MESH,
        )

    def send_memory(s, c):
        return pltpu.make_async_remote_copy(
            src_ref=sent_rows.at[c],
            dst_ref=got_rows.at[c],
            send_sem=mem_send.at[s - half, c],
            recv_sem=mem_recv.at[c],
            device_id={"segment": s},
            device_id_type=MESH,
        )

    for off in range(1, split):
        send_acts(off).start()
    own_acts.wait()
    gain_copy.wait()
    final_copy.wait()
    for off in range(1, split):
        send_acts(off).wait_recv()

    tokens = gathered[...].reshape(rows, features).astype(F32)
    scale = lax.rsqrt(jnp.mean(tokens * tokens, axis=-1, keepdims=True) + EPSILON)
    normed[...] = (tokens * scale * gain_buf[...]).astype(BF16)

    def attend(queries, keys, values):
        results = []
        for h in range(wide // HDIM):
            cols = slice(h * HDIM, (h + 1) * HDIM)
            scores = lax.dot_general(
                queries[:, cols], keys[:, cols], (((1,), (1,)), ((), ())), preferred_element_type=F32
            )
            weights = jnp.exp(scores)
            probs = (weights / jnp.sum(weights, axis=-1, keepdims=True)).astype(BF16)
            results.append(jnp.dot(probs, values[:, cols], preferred_element_type=F32).astype(BF16))
        return jnp.concatenate(results, axis=1)

    @pl.when(encoder)
    def _():
        def group(j, carry):
            source = normed[...]
            load_q(j).wait()
            queries = jnp.dot(source, query_buf[j], preferred_element_type=F32).astype(BF16)
            load_k(j).wait()
            keys = jnp.dot(source, key_buf[j], preferred_element_type=F32).astype(BF16)
            load_v(j).wait()
            values = jnp.dot(source, value_buf[j], preferred_element_type=F32).astype(BF16)
            fresh[0, 0, :, columns(j)] = keys
            fresh[0, 1, :, columns(j)] = values
            context[:, columns(j)] = attend(queries, keys, values)
            return carry

        lax.fori_loop(0, groups, group, 0)

    @pl.when(decoder)
    def _():
        cache_copy.wait()

        def group(j, carry):
            load_q(j).wait()
            queries = jnp.dot(normed[...], query_buf[j], preferred_element_type=F32).astype(BF16)
            context[:, columns(j)] = attend(queries, cache_buf[0, :, columns(j)], cache_buf[1, :, columns(j)])
            return carry

        lax.fori_loop(0, groups, group, 0)

    def project(c):
        load_out(c).wait()
        made = jnp.dot(context[...], out_buf[c], preferred_element_type=F32).astype(BF16)
        own_part[c] = made.reshape(parts, local_rows, narrow)

        @pl.when(is_root)
        def _():
            for off in range(1, split):
                send_all_rows(off, c).start()

        @pl.when(not_root)
        def _():
            for off in range(1, split):
                send_their_rows(off, c).start()

    def combine(c):
        cols = slice(c * narrow, (c + 1) * narrow)

        @pl.when(is_root)
        def _():
            for off in range(1, split):
                send_all_rows(off, c).wait_recv()
            branch = own_part[c].astype(F32)
            for off in range(1, split):
                branch = branch + got_part[off - 1, c].astype(F32)
            sent_rows[c] = (gathered[:, :, cols].astype(F32) + branch).astype(BF16)
            for s in range(half, sections):
                send_memory(s, c).start()
            updated[0, :, cols] = sent_rows[c, me]

        @pl.when(not_root)
        def _():
            for off in range(1, split):
                send_their_rows(off, c).wait_recv()
            branch = own_part[c, me].astype(F32)
            for off in range(1, split):
                branch = branch + got_part[off - 1, c, me].astype(F32)
            updated[0, :, cols] = (gathered[me, :, cols].astype(F32) + branch).astype(BF16)

    lag = min(2, blocks - 1)
    for c in range(blocks):
        project(c)
        if c >= lag:
            combine(c - lag)
    for c in range(blocks - lag, blocks):
        combine(c)

    @pl.when(decoder)
    def _():
        def arrive(j, carry):
            load_k(j).wait()
            load_v(j).wait()
            return carry

        lax.fori_loop(0, groups, arrive, 0)
        squares = jnp.zeros((rows, 1), F32)
        for c in range(blocks):
            cols = slice(c * narrow, (c + 1) * narrow)
            send_memory(half, c).wait_recv()
            memory = got_rows[c].reshape(rows, narrow).astype(F32)
            squares = squares + jnp.sum(memory * memory, axis=-1, keepdims=True)
            source = (memory * final_buf[:, cols]).astype(BF16)
            last = c == blocks - 1
            if last:
                scale = lax.rsqrt(squares * (1.0 / features) + EPSILON)

            def group(j, carry):
                for which, weights in ((0, key_buf), (1, value_buf)):
                    term = jnp.dot(source, weights[j, cols, :], preferred_element_type=F32)
                    if c > 0:
                        term = term + total[which, j]
                    if last:
                        fresh[0, which, :, columns(j)] = (term * scale).astype(BF16)
                    else:
                        total[which, j] = term
                return carry

            lax.fori_loop(0, groups, group, 0)

    for off in range(1, split):
        send_acts(off).wait_send()

    @pl.when(is_root)
    def _():
        for c in range(blocks):
            for off in range(1, split):
                send_all_rows(off, c).wait_send()
            for s in range(half, sections):
                send_memory(s, c).wait_send()

    @pl.when(not_root)
    def _():
        for c in range(blocks):
            for off in range(1, split):
                send_their_rows(off, c).wait_send()


def solution(mesh):
    sections, split = mesh.shape["segment"], mesh.shape["tensor"]

    def on_device(acts, norm_gain, final_gain, w_query, w_key, w_value, w_out, cache):
        local_rows, features = acts.shape[1:]
        inner = w_query.shape[2]
        rows = split * local_rows
        wide = largest(inner, 512)
        narrow = largest(features, 256)
        groups, blocks = inner // wide, features // narrow
        dma = pltpu.SemaphoreType.DMA
        return pl.pallas_call(
            functools.partial(kernel, sections, split, wide, narrow),
            out_shape=(
                jax.ShapeDtypeStruct(acts.shape, BF16),
                jax.ShapeDtypeStruct(cache.shape, BF16),
            ),
            in_specs=[pl.BlockSpec(memory_space=pltpu.HBM)] * 8,
            out_specs=(pl.BlockSpec(memory_space=pltpu.VMEM), pl.BlockSpec(memory_space=pltpu.VMEM)),
            scratch_shapes=[
                pltpu.VMEM((groups, features, wide), BF16),
                pltpu.VMEM((groups, features, wide), BF16),
                pltpu.VMEM((groups, features, wide), BF16),
                pltpu.VMEM((blocks, inner, narrow), BF16),
                pltpu.VMEM((2, rows, inner), BF16),
                pltpu.VMEM((1, features), F32),
                pltpu.VMEM((1, features), F32),
                pltpu.VMEM((split, local_rows, features), BF16),
                pltpu.VMEM((rows, features), BF16),
                pltpu.VMEM((rows, inner), BF16),
                pltpu.VMEM((blocks, split, local_rows, narrow), BF16),
                pltpu.VMEM((split - 1, blocks, split, local_rows, narrow), BF16),
                pltpu.VMEM((blocks, split, local_rows, narrow), BF16),
                pltpu.VMEM((blocks, split, local_rows, narrow), BF16),
                pltpu.VMEM((2, groups, rows, wide), F32),
                dma((3, groups)),
                dma((blocks,)),
                dma((4,)),
                dma((split - 1,)),
                dma((split - 1,)),
                dma((split - 1, blocks)),
                dma((split - 1, blocks)),
                dma((sections - sections // 2, blocks)),
                dma((blocks,)),
            ],
            compiler_params=pltpu.CompilerParams(
                collective_id=0, has_side_effects=True, vmem_limit_bytes=58 * 1024 * 1024
            ),
        )(acts, norm_gain, final_gain.reshape(1, features), w_query, w_key, w_value, w_out, cache)

    placed = (
        P("segment", ("dp", "tensor"), None),
        P("segment", None),
        P(),
        P("segment", None, "tensor"),
        P("segment", None, "tensor"),
        P("segment", None, "tensor"),
        P("segment", "tensor", None),
        P("segment", None, "dp", "tensor"),
    )
    return jax.shard_map(
        on_device,
        mesh=mesh,
        in_specs=placed,
        out_specs=(P("segment", ("dp", "tensor"), None), P("segment", None, "dp", "tensor")),
        check_vma=False,
    )
```

time: 78.7 us -> 35.4 us (0.45)
  the two profiles are of different devices: /device:TPU:2 before, /device:TPU:19 now
where the time goes in v1:
time: 35.4 us; the launch traced here: 35.2 us
  Pallas kernels  30.8 us (87%)
  local copies, waits for them, and re-layouts  3.76 us (11%)
  between operations  0.64 us (2%)
    pallas_call x1, Pallas kernels, on_device(): pl.pallas_call(functools.partial(kernel, sections, split, wide, narrow),...  30.8 us
    unnamed x2, local copies, waits for them, and re-layouts  3.76 us

profile of v1, /device:TPU:19, one launch (start us, length us, event | category | flops | bytes accessed | tf_op | source)
XLA Modules:
  0.0 35.2 jit_solution(15806985718667562467)
XLA Ops:
  0.6 30.8 %shard_map.95 = (bf16[1,32,1024]{2,1,0:T(8,128)(2,1)}, bf16[1,2,64,4096]{3,2,1,0:T(8,128)(2,1)}) custom-call(bf16[1,32,1024]{2,1,0:T(8,128)(2,1)} %acts.1, f32[1,1024]{1,0:T(1,128)} %norm_gain.1, f32[1,1024]{1,0:T(1,128)} %bitcast.1, bf16[1,1024,4096]{2,1,0:T(8,128)(2,1)} %w_query.1, bf16[1,1024,4096]{2,1,0:T(8,128)(2,1)} %w_key.1, ...), custom_call_target="tpu_custom_call" | custom-call | tf_op jit(solution)/shard_map/pallas_call | solution.py:330
  31.5 1.5 %copy.12 = bf16[1,32,1024]{2,1,0:T(8,128)(2,1)} copy(bf16[1,32,1024]{2,1,0:T(8,128)(2,1)} %get-tuple-element.4) | data formatting | bytes 131072
  32.9 2.3 %copy.13 = bf16[1,2,64,4096]{3,2,1,0:T(8,128)(2,1)} copy(bf16[1,2,64,4096]{3,2,1,0:T(8,128)(2,1)} %get-tuple-element.5) | data formatting | bytes 2097152

commit v2 on v1

--- a/solution.py
+++ b/solution.py
@@ -12,6 +12,7 @@
 MESH = pl.DeviceIdType.MESH
 F32 = jnp.float32
 BF16 = jnp.bfloat16
+LARGEST = float(jnp.finfo(jnp.bfloat16).max)
 
 
 def largest(total, limit):
@@ -26,7 +27,7 @@
     acts, norm_gain, final_gain, w_query, w_key, w_value, w_out, cache,
     updated, fresh,
     query_buf, key_buf, value_buf, out_buf, cache_buf, gain_buf, final_buf,
-    gathered, normed, context, own_part, got_part, sent_rows, got_rows, total,
+    gathered, normed, context, own_part, got_part, sent_rows, got_rows, total, slots, same_head,
     qkv_sem, out_sem, small_sem, act_send, act_recv, part_send, part_recv, mem_send, mem_recv,
 ):
     segment = lax.axis_index("segment")
@@ -178,46 +179,88 @@
     scale = lax.rsqrt(jnp.mean(tokens * tokens, axis=-1, keepdims=True) + EPSILON)
     normed[...] = (tokens * scale * gain_buf[...]).astype(BF16)
 
+    which_row = lax.broadcasted_iota(jnp.int32, same_head.shape, 0) < rows
+    which_column = lax.broadcasted_iota(jnp.int32, same_head.shape, 1) < rows
+    same_head[...] = jnp.where(which_row == which_column, 1.0, 0.0).astype(BF16)
+
     def attend(queries, keys, values):
-        results = []
-        for h in range(wide // HDIM):
-            cols = slice(h * HDIM, (h + 1) * HDIM)
-            scores = lax.dot_general(
-                queries[:, cols], keys[:, cols], (((1,), (1,)), ((), ())), preferred_element_type=F32
+        blank = jnp.zeros((rows, HDIM), BF16)
+        pairs = wide // (2 * HDIM)
+
+        def spread(source, p):
+            first = source[:, 2 * p * HDIM : (2 * p + 1) * HDIM]
+            second = source[:, (2 * p + 1) * HDIM : (2 * p + 2) * HDIM]
+            return jnp.concatenate(
+                [jnp.concatenate([first, blank], axis=1), jnp.concatenate([blank, second], axis=1)], axis=0
             )
-            weights = jnp.exp(scores)
-            probs = (weights / jnp.sum(weights, axis=-1, keepdims=True)).astype(BF16)
-            results.append(jnp.dot(probs, values[:, cols], preferred_element_type=F32).astype(BF16))
+
+        scores = [
+            lax.dot_general(
+                queries[:, 2 * p * HDIM : (2 * p + 2) * HDIM], spread(keys, p),
+                (((1,), (1,)), ((), ())), preferred_element_type=F32,
+            )
+            for p in range(pairs)
+        ]
+        weights = [jnp.minimum(jnp.exp(score), LARGEST) for score in scores]
+        ones = same_head[...]
+        sums = [jnp.dot(weight.astype(BF16), ones, preferred_element_type=F32) for weight in weights]
+        probs = [(weight / total_of).astype(BF16) for weight, total_of in zip(weights, sums)]
+        results = [
+            jnp.dot(probs[p], spread(values, p), preferred_element_type=F32).astype(BF16) for p in range(pairs)
+        ]
         return jnp.concatenate(results, axis=1)
 
+    def attend_slot(slot, j):
+        context[:, columns(j)] = attend(slots[slot, 0], slots[slot, 1], slots[slot, 2])
+
+    def own_group(slot, j):
+        source = normed[...]
+        for which, weights in ((0, query_buf), (1, key_buf), (2, value_buf)):
+            made = jnp.dot(source, weights[j], preferred_element_type=F32).astype(BF16)
+            slots[slot, which] = made
+            if which > 0:
+                fresh[0, which - 1, :, columns(j)] = made
+
+    def cached_group(slot, j):
+        made = jnp.dot(normed[...], query_buf[j], preferred_element_type=F32).astype(BF16)
+        slots[slot, 0] = made
+        slots[slot, 1] = cache_buf[0, :, columns(j)]
+        slots[slot, 2] = cache_buf[1, :, columns(j)]
+
+    def pipelined(wait, make):
+        wait(0)
+        make(0, 0)
+
+        def pair(i, carry):
+            j = 2 * i + 1
+            wait(j)
+            attend_slot(0, j - 1)
+            make(1, j)
+            wait(j + 1)
+            attend_slot(1, j)
+            make(0, j + 1)
+            return carry
+
+        lax.fori_loop(0, (groups - 1) // 2, pair, 0)
+        if groups % 2 == 0:
+            wait(groups - 1)
+            attend_slot(0, groups - 2)
+            make(1, groups - 1)
+        attend_slot((groups - 1) % 2, groups - 1)
+
     @pl.when(encoder)
     def _():
-        def group(j, carry):
-            source = normed[...]
+        def wait(j):
             load_q(j).wait()
-            queries = jnp.dot(source, query_buf[j], preferred_element_type=F32).astype(BF16)
             load_k(j).wait()
-            keys = jnp.dot(source, key_buf[j], preferred_element_type=F32).astype(BF16)
             load_v(j).wait()
-            values = jnp.dot(source, value_buf[j], preferred_element_type=F32).astype(BF16)
-            fresh[0, 0, :, columns(j)] = keys
-            fresh[0, 1, :, columns(j)] = values
-            context[:, columns(j)] = attend(queries, keys, values)
-            return carry
-
-        lax.fori_loop(0, groups, group, 0)
+
+        pipelined(wait, own_group)
 
     @pl.when(decoder)
     def _():
         cache_copy.wait()
-
-        def group(j, carry):
-            load_q(j).wait()
-            queries = jnp.dot(normed[...], query_buf[j], preferred_element_type=F32).astype(BF16)
-            context[:, columns(j)] = attend(queries, cache_buf[0, :, columns(j)], cache_buf[1, :, columns(j)])
-            return carry
-
-        lax.fori_loop(0, groups, group, 0)
+        pipelined(lambda j: load_q(j).wait(), cached_group)
 
     def project(c):
         load_out(c).wait()
@@ -323,16 +366,13 @@
         local_rows, features = acts.shape[1:]
         inner = w_query.shape[2]
         rows = split * local_rows
-        wide = largest(inner, 512)
+        wide = largest(inner, 1024)
         narrow = largest(features, 256)
         groups, blocks = inner // wide, features // narrow
         dma = pltpu.SemaphoreType.DMA
         return pl.pallas_call(
             functools.partial(kernel, sections, split, wide, narrow),
-            out_shape=(
-                jax.ShapeDtypeStruct(acts.shape, BF16),
-                jax.ShapeDtypeStruct(cache.shape, BF16),
-            ),
+            out_shape=(pltpu.VMEM(acts.shape, BF16), pltpu.VMEM(cache.shape, BF16)),
             in_specs=[pl.BlockSpec(memory_space=pltpu.HBM)] * 8,
             out_specs=(pl.BlockSpec(memory_space=pltpu.VMEM), pl.BlockSpec(memory_space=pltpu.VMEM)),
             scratch_shapes=[
@@ -351,6 +391,8 @@
                 pltpu.VMEM((blocks, split, local_rows, narrow), BF16),
                 pltpu.VMEM((blocks, split, local_rows, narrow), BF16),
                 pltpu.VMEM((2, groups, rows, wide), F32),
+                pltpu.VMEM((2, 3, rows, wide), BF16),
+                pltpu.VMEM((2 * rows, 2 * rows), BF16),
                 dma((3, groups)),
                 dma((blocks,)),
                 dma((4,)),

time: 35.4 us -> 23.8 us (0.67)
  Pallas kernels: 30.8 us -> 21.4 us
  local copies, waits for them, and re-layouts: 3.76 us -> 1.6 us
    pallas_call x1, Pallas kernels: 30.8 us -> 21.4 us  [on_device(): pl.pallas_call(functools.partial(kernel, sections, split, wide, narrow),...]
    unnamed x2, local copies, waits for them, and re-layouts: 3.76 us -> 1.6 us
where the time goes in v2:
time: 23.8 us; the launch traced here: 23.6 us
  Pallas kernels  21.4 us (90%)
  local copies, waits for them, and re-layouts  1.6 us (7%)
  between operations  0.64 us (3%)
    pallas_call x1, Pallas kernels, on_device(): pl.pallas_call(functools.partial(kernel, sections, split, wide, narrow),...  21.4 us
    unnamed x2, local copies, waits for them, and re-layouts  1.6 us

profile of v2, /device:TPU:19, one launch (start us, length us, event | category | flops | bytes accessed | tf_op | source)
XLA Modules:
  0.0 23.6 jit_solution(891590267527958968)
XLA Ops:
  0.6 21.4 %shard_map.95 = (bf16[1,32,1024]{2,1,0:T(8,128)(2,1)S(1)}, bf16[1,2,64,4096]{3,2,1,0:T(8,128)(2,1)S(1)}) custom-call(bf16[1,32,1024]{2,1,0:T(8,128)(2,1)} %acts.1, f32[1,1024]{1,0:T(1,128)} %norm_gain.1, f32[1,1024]{1,0:T(1,128)} %bitcast.1, bf16[1,1024,4096]{2,1,0:T(8,128)(2,1)} %w_query.1, bf16[1,1024,4096]{2,1,0:T(8,128)(2,1)} %w_key.1, ...), custom_call_target="tpu_custom_call" | custom-call | tf_op jit(solution)/shard_map/pallas_call | solution.py:373
  22.0 0.6 %copy.12 = bf16[1,32,1024]{2,1,0:T(8,128)(2,1)} copy(bf16[1,32,1024]{2,1,0:T(8,128)(2,1)S(1)} %get-tuple-element.2) | data formatting | bytes 131072
  22.7 1.0 %copy.13 = bf16[1,2,64,4096]{3,2,1,0:T(8,128)(2,1)} copy(bf16[1,2,64,4096]{3,2,1,0:T(8,128)(2,1)S(1)} %get-tuple-element.3) | data formatting | bytes 2097152

commit v3 on v2

--- a/solution.py
+++ b/solution.py
@@ -339,7 +339,7 @@
                         total[which, j] = term
                 return carry
 
-            lax.fori_loop(0, groups, group, 0)
+            lax.fori_loop(0, groups, group, 0, unroll=True)
 
     for off in range(1, split):
         send_acts(off).wait_send()

time: 23.8 us -> 22.7 us (0.954)
  Pallas kernels: 21.4 us -> 20.3 us
    pallas_call x1, Pallas kernels: 21.4 us -> 20.3 us  [on_device(): pl.pallas_call(functools.partial(kernel, sections, split, wide, narrow),...]
where the time goes in v3:
time: 22.7 us; the launch traced here: 22.5 us
  Pallas kernels  20.3 us (89%)
  local copies, waits for them, and re-layouts  1.6 us (7%)
  between operations  0.64 us (3%)
    pallas_call x1, Pallas kernels, on_device(): pl.pallas_call(functools.partial(kernel, sections, split, wide, narrow),...  20.3 us
    unnamed x2, local copies, waits for them, and re-layouts  1.6 us

profile of v3, /device:TPU:19, one launch (start us, length us, event | category | flops | bytes accessed | tf_op | source)
XLA Modules:
  0.0 22.5 jit_solution(16420094501659042557)
XLA Ops:
  0.6 20.3 %shard_map.95 = (bf16[1,32,1024]{2,1,0:T(8,128)(2,1)S(1)}, bf16[1,2,64,4096]{3,2,1,0:T(8,128)(2,1)S(1)}) custom-call(bf16[1,32,1024]{2,1,0:T(8,128)(2,1)} %acts.1, f32[1,1024]{1,0:T(1,128)} %norm_gain.1, f32[1,1024]{1,0:T(1,128)} %bitcast.1, bf16[1,1024,4096]{2,1,0:T(8,128)(2,1)} %w_query.1, bf16[1,1024,4096]{2,1,0:T(8,128)(2,1)} %w_key.1, ...), custom_call_target="tpu_custom_call" | custom-call | tf_op jit(solution)/shard_map/pallas_call | solution.py:373
  20.9 0.6 %copy.12 = bf16[1,32,1024]{2,1,0:T(8,128)(2,1)} copy(bf16[1,32,1024]{2,1,0:T(8,128)(2,1)S(1)} %get-tuple-element.2) | data formatting | bytes 131072
  21.6 1.0 %copy.13 = bf16[1,2,64,4096]{3,2,1,0:T(8,128)(2,1)} copy(bf16[1,2,64,4096]{3,2,1,0:T(8,128)(2,1)S(1)} %get-tuple-element.3) | data formatting | bytes 2097152
